TPU v7x, 512 devices: a whole 4x8x8 slice. The times are simulated.
512 devices in a mesh: tm: 16 (over x, z_hi, core), contact: 32 (over z_lo, y).
Axes of the slice: x: 4, y: 8, z: 8 (z_hi: 2, z_lo: 4; z = z_hi * 4 + z_lo), core: 2. Of those that a mesh axis runs over, the one named last changes fastest.
Arguments:
- signal: bfloat16 [8, 512, 16384], P(None, 'contact', 'tm'), may hold values from -6 to 6
- fir_taps: bfloat16 [512, 129], P('contact'), may hold values from -0.5 to 0.5
- neighbours: int32 [512, 4], replicated, may hold values from 0 to 511, as said below
- live_mask: int32 [512], replicated, may hold values 0 or 1
- lap_coef: float32 [512], replicated, may hold values from 0.1 to 1
- w_query: bfloat16 [256, 256], replicated, may hold values from -8 to 8
- w_key: bfloat16 [256, 256], replicated, may hold values from -8 to 8
- w_value: bfloat16 [256, 256], replicated, may hold values from -0.375 to 0.375
- w_out: bfloat16 [256, 256], replicated, may hold values from -0.375 to 0.375
- cotangent: bfloat16 [8, 512, 16384], P(None, 'contact', 'tm'), may hold values from -6 to 6
Outputs:
- attended: bfloat16 [8, 512, 16384], P(None, 'contact', 'tm')
- weight_grads: float32 [4, 256, 256], replicated
Inputs may be any that keep to these rules, and one draw needn't show every extreme that they name: `neighbours`: entry [c, k] names a contact whose grid row (index // 16) differs from that of contact c by at most one and whose column (index % 16) differs by at most two.
All inputs are finite; a program needn't handle non-finite values.
Results may differ from a plain program's by a relative error of at most 0.011.
Values may be sent and summed in bfloat16 or wider, within the bound.
A program may use at most 64 MiB of HBM per device.

v0:
```python
import jax
import jax.numpy as jnp
from jax import lax
from jax.sharding import PartitionSpec as P

GRID_COLS = 16
HEADS = 4


def from_behind(value, axis, by):
    count = lax.axis_size(axis)
    pairs = [(i, i + by) for i in range(count) if 0 <= i + by < count]
    return lax.ppermute(value, axis, pairs)


def extended_2(cells, sides, width):
    for axis, dim in sides:
        count = lax.axis_size(axis)
        ends = count - 1
        head = lax.slice_in_dim(cells, 0, width, axis=dim)
        tail = lax.slice_in_dim(cells, cells.shape[dim] - width, cells.shape[dim], axis=dim)
        cells = jnp.concatenate(
            [
                lax.ppermute(tail, axis, [(i, (i + 1) % count) for i in range(ends)]),
                cells,
                lax.ppermute(head, axis, [((i + 1) % count, i) for i in range(ends)]),
            ],
            axis=dim,
        )
    return cells


def contract(left, right, left_dim, right_dim):
    return lax.dot_general(
        left, right, (((left_dim,), (right_dim,)), ((), ())), preferred_element_type=jnp.float32
    )


def toeplitz(fir_taps):
    rim_width = fir_taps.shape[1] - 1
    source = jnp.arange(2 * rim_width, dtype=jnp.int32)[:, None]
    target = jnp.arange(rim_width, dtype=jnp.int32)[None, :]
    lag_table = target + rim_width - source
    inside = (lag_table >= 0) & (lag_table <= rim_width)
    picked = jnp.take(fir_taps, jnp.clip(lag_table, 0, rim_width), axis=1)
    return jnp.where(inside[None, :, :], picked, jnp.zeros_like(picked))


def laplace(field, centre, indices, nbr_alive, own_alive, coef):
    source_ids = jnp.arange(field.shape[-2], dtype=jnp.int32)
    counts = jnp.zeros((indices.shape[0], field.shape[-2]), jnp.float32)
    for slot_index in range(indices.shape[1]):
        hit = (indices[:, slot_index][:, None] == source_ids[None, :]).astype(jnp.float32)
        counts = counts + nbr_alive[:, slot_index][:, None] * hit
    alive_count = jnp.sum(nbr_alive, axis=1)
    beside = jnp.einsum(
        "cn,bnt->bct", counts.astype(jnp.bfloat16), field, preferred_element_type=jnp.float32
    )
    middle = centre.astype(jnp.float32)
    running = beside - alive_count[:, None] * middle
    return (own_alive[:, None] * (middle + coef[:, None] * running)).astype(jnp.bfloat16)


def one_head(query_head, key_head, value_head, back_head, key_alive, score_scale):
    scores = contract(query_head, key_head, 1, 1) * score_scale
    scores = jnp.where(key_alive[None, :] > 0, scores, -1e30)
    top_score = jnp.max(scores, axis=1, keepdims=True)
    raised = jnp.exp(scores - top_score)
    attn_prob = raised / jnp.sum(raised, axis=1, keepdims=True)
    prob_low = attn_prob.astype(jnp.bfloat16)
    head_out = jnp.dot(prob_low, value_head, preferred_element_type=jnp.float32).astype(
        jnp.bfloat16
    )
    grad_value = contract(prob_low, back_head, 0, 0).astype(jnp.bfloat16)
    grad_prob = contract(back_head, value_head, 1, 1)
    row_inner = jnp.sum(
        back_head.astype(jnp.float32) * head_out.astype(jnp.float32), axis=1, keepdims=True
    )
    grad_score = (attn_prob * (grad_prob - row_inner) * score_scale).astype(jnp.bfloat16)
    grad_query = jnp.dot(grad_score, key_head, preferred_element_type=jnp.float32).astype(
        jnp.bfloat16
    )
    grad_key = contract(grad_score, query_head, 0, 0).astype(jnp.bfloat16)
    return (head_out, grad_query, grad_key, grad_value)


def group_step(tokens, upstream, key_alive, w_query, w_key, w_value, w_out):
    as_float = tokens.astype(jnp.float32)
    normed = (
        as_float * lax.rsqrt(jnp.mean(as_float * as_float, axis=1, keepdims=True) + 1e-05)
    ).astype(jnp.bfloat16)
    query_rows = jnp.dot(normed, w_query, preferred_element_type=jnp.float32).astype(jnp.bfloat16)
    key_rows = jnp.dot(normed, w_key, preferred_element_type=jnp.float32).astype(jnp.bfloat16)
    value_rows = jnp.dot(normed, w_value, preferred_element_type=jnp.float32).astype(jnp.bfloat16)
    back_signal = contract(upstream, w_out, 1, 1).astype(jnp.bfloat16)
    head_size = w_query.shape[1] // HEADS
    score_scale = head_size ** (-0.5)
    head_results = []
    for head_index in range(HEADS):
        lower = head_index * head_size
        upper = lower + head_size
        head_results.append(
            one_head(
                query_rows[:, lower:upper],
                key_rows[:, lower:upper],
                value_rows[:, lower:upper],
                back_signal[:, lower:upper],
                key_alive,
                score_scale,
            )
        )
    mixed_heads = jnp.concatenate([entry[0] for entry in head_results], axis=1)
    grad_query = jnp.concatenate([entry[1] for entry in head_results], axis=1)
    grad_key = jnp.concatenate([entry[2] for entry in head_results], axis=1)
    grad_value = jnp.concatenate([entry[3] for entry in head_results], axis=1)
    attended = jnp.dot(mixed_heads, w_out, preferred_element_type=jnp.float32).astype(jnp.bfloat16)
    grad_stack = jnp.stack(
        [
            contract(normed, grad_query, 0, 0),
            contract(normed, grad_key, 0, 0),
            contract(normed, grad_value, 0, 0),
            contract(mixed_heads, upstream, 0, 0),
        ]
    )
    return (attended, grad_stack)


def to_groups(whole, patch_len):
    batch_size, contacts_here, slab_len = whole.shape
    patch_count = slab_len // patch_len
    shaped = whole.reshape(batch_size, contacts_here, patch_count, patch_len).transpose(0, 2, 1, 3)
    return shaped.reshape(batch_size * patch_count, contacts_here, patch_len)


def from_groups(grouped, batch_size):
    group_count, contacts_here, patch_len = grouped.shape
    patch_count = group_count // batch_size
    shaped = grouped.reshape(batch_size, patch_count, contacts_here, patch_len).transpose(
        0, 2, 1, 3
    )
    return shaped.reshape(batch_size, contacts_here, patch_count * patch_len)


def local(
    signal, fir_taps, neighbours, live_mask, lap_coef, w_query, w_key, w_value, w_out, cotangent
):
    batch_size, contacts_here, slab_len = signal.shape
    rim_width = fir_taps.shape[1] - 1
    patch_len = w_query.shape[0]
    patch_count = slab_len // patch_len
    prior_rim = from_behind(signal[:, :, slab_len - rim_width :], "tm", 1)
    extended = jnp.concatenate([prior_rim, signal], axis=2)
    blocks = extended.reshape(batch_size, contacts_here, slab_len // rim_width + 1, rim_width)
    windows = jnp.concatenate([blocks[:, :, :-1], blocks[:, :, 1:]], axis=3)
    filter_table = toeplitz(fir_taps)
    filtered = jnp.einsum(
        "bcjw,cwu->bcju", windows, filter_table, preferred_element_type=jnp.float32
    )
    filtered = filtered.reshape(batch_size, contacts_here, slab_len).astype(jnp.bfloat16)
    alive_f = live_mask.astype(jnp.float32)
    nbr_alive = jnp.take(alive_f, neighbours)
    first_contact = lax.axis_index("contact") * contacts_here
    padded = extended_2(filtered, (("contact", 1),), GRID_COLS)
    local_index = (
        lax.dynamic_slice_in_dim(neighbours, first_contact, contacts_here, 0)
        - first_contact
        + GRID_COLS
    )
    ready = laplace(
        padded,
        filtered,
        local_index,
        lax.dynamic_slice_in_dim(nbr_alive, first_contact, contacts_here, 0),
        lax.dynamic_slice_in_dim(alive_f, first_contact, contacts_here, 0),
        lax.dynamic_slice_in_dim(lap_coef, first_contact, contacts_here, 0),
    )
    grouped = to_groups(ready, patch_len)
    features, upstream = (
        lax.all_to_all(grouped, "contact", split_axis=0, concat_axis=1, tiled=True),
        lax.all_to_all(
            to_groups(cotangent, patch_len), "contact", split_axis=0, concat_axis=1, tiled=True
        ),
    )

    def run_group(running, inputs_pair):
        attended, grad_stack = group_step(
            inputs_pair[0], inputs_pair[1], alive_f, w_query, w_key, w_value, w_out
        )
        return (running + grad_stack, attended)

    running, attended_groups = lax.scan(
        run_group, jnp.zeros((4, patch_len, patch_len), jnp.float32), (features, upstream)
    )
    summed = lax.psum(running, ("tm", "contact"))
    returned = lax.all_to_all(attended_groups, "contact", split_axis=1, concat_axis=0, tiled=True)
    attended = from_groups(returned, batch_size)
    grad_scale = (batch_size * patch_count * lax.axis_size("tm") * neighbours.shape[0]) ** (-0.5)
    return (attended, summed * grad_scale)


def solution(mesh):
    in_specs = (
        P(None, "contact", "tm"),
        P("contact", None),
        P(),
        P(),
        P(),
        P(),
        P(),
        P(),
        P(),
        P(None, "contact", "tm"),
    )
    out_specs = (P(None, "contact", "tm"), P())
    return jax.shard_map(local, mesh=mesh, in_specs=in_specs, out_specs=out_specs, check_vma=False)
```

profile of v0, /device:TPU:24, one launch (start us, length us, event | category | flops | bytes accessed | tf_op | source)
XLA Modules:
  0.0 490.5 jit_solution(11078941743470237049)
XLA Ops:
  7.2 0.8 slice.121
  8.0 1.7 collective-permute-start
  9.7 1.0 fusion.132
  10.7 0.7 pad_maximum_fusion.5
  11.4 12.9 %all-to-all-start.2 = ((bf16[32,16,256]{2,1,0:T(8,128)(2,1)}), bf16[32,16,256]{2,1,0:T(8,128)(2,1)S(1)}, u32[]{:S(2)}, u32[]{:S(2)}) async-start(bf16[32,16,256]{2,1,0:T(8,128)(2,1)} %bitcast.20), calls=%async_computation.2 | async-start | bytes 524288 | tf_op jit(solution)/shard_map/all_to_all | solution.py:180
  24.9 13.2 %gather_fusion.1 = f32[2048]{0:T(1024)S(1)} fusion(f32[512]{0:T(512)S(1)} %convert_element_type.188, s32[2048]{0:T(1024)S(1)} %broadcast_clamp_fusion), kind=kCustom, calls=%fused_computation.1 | custom fusion | bytes 24576 | tf_op jit(solution)/shard_map/jit(_take)/gather | solution.py:161
  38.7 114.2 %gather_fusion = bf16[32768,16]{1,0:T(8,128)(2,1)} fusion(bf16[16,129]{0,1:T(8,128)(2,1)S(1)} %copy.116, s32[32768]{0:T(1024)S(1)} %fusion.71), kind=kCustom, calls=%fused_computation | custom fusion | bytes 2228224 | tf_op jit(solution)/shard_map/jit(_take)/gather | solution.py:45
  152.9 6.9 %copy.117 = bf16[256,128,16]{1,0,2:T(8,128)(2,1)S(1)} copy(bf16[256,128,16]{2,1,0:T(8,128)(2,1)} %bitcast.104) | data formatting | bytes 2097152 | tf_op jit(solution)/shard_map/jit(_take)/gather | solution.py:45
  160.1 0.4 fusion.22
  160.8 2.5 collective-permute-start.2
  163.3 4.6 collective-permute-start.1
  168.0 0.8 dynamic_slice.18
  168.8 1.5 collective-permute-done.2
  170.3 1.5 collective-permute-done.1
  171.7 0.3 fusion.20
  172.1 0.7 pad_maximum_fusion.3
  172.9 11.1 %all-to-all-start = ((bf16[32,16,256]{2,1,0:T(8,128)(2,1)}), bf16[32,16,256]{2,1,0:T(8,128)(2,1)S(1)}, u32[]{:S(2)}, u32[]{:S(2)}) async-start(bf16[32,16,256]{2,1,0:T(8,128)(2,1)} %bitcast.16), calls=%async_computation | async-start | bytes 524288 | tf_op jit(solution)/shard_map/all_to_all | solution.py:179
  184.5 9.0 %all-to-all-done = bf16[32,16,256]{2,1,0:T(8,128)(2,1)S(1)} async-done(((bf16[32,16,256]{2,1,0:T(8,128)(2,1)}), bf16[32,16,256]{2,1,0:T(8,128)(2,1)S(1)}, u32[]{:S(2)}, u32[]{:S(2)}) %all-to-all-start) | async-done | bytes 262176 | tf_op jit(solution)/shard_map/all_to_all | solution.py:179
  193.9 0.3 convolution_convert_fusion.3
  194.5 0.4 fusion.134
  194.8 0.4 fusion.135
  195.2 0.4 fusion.136
  195.6 0.4 fusion.137
  196.3 0.5 copy-done.4
  197.9 0.3 convolution_convert_fusion.14
  198.2 0.3 convolution_convert_fusion.15
  199.1 0.3 convolution_convert_fusion.16
  199.7 0.3 convolution_convert_fusion.17
  200.3 0.4 fusion.12
  200.7 0.3 convolution_convert_fusion.18
  201.2 0.4 fusion.13
  201.6 0.3 convolution_convert_fusion.19
  202.1 0.4 fusion.14
  202.5 0.3 convolution_convert_fusion.20
  203.0 0.4 fusion.15
  203.4 0.3 convolution_convert_fusion.21
  204.1 0.3 convolution_bitcast_fusion.2
  204.4 0.3 convolution_bitcast_fusion.3
  204.7 0.3 convolution_bitcast_fusion.4
  204.9 1.0 pad_maximum_fusion
  206.3 0.4 copy.146
  206.7 0.5 broadcast.198
  207.2 2.2 reduce.4
  209.5 15.4 %all_to_all.12 = bf16[32,2,2048]{2,1,0:T(2,128)(2,1)S(1)} all-to-all(bf16[32,2,2048]{2,1,0:T(2,128)(2,1)S(1)} %reshape.193), channel_id=1, replica_groups=mesh['tm'=16,'contact'=32] {'contact'}, dimensions={0} | all-to-all | bytes 524288 | tf_op jit(solution)/shard_map/all_to_all | solution.py:195
  224.9 0.3 reshape.194
  225.2 0.7 copy.142
  226.0 255.4 %all-reduce.2.cloned.1.call-done = f32[4,256,256]{2,1,0:T(8,128)} async-done(((f32[4,256,256]{2,1,0:T(8,128)}), f32[4,256,256]{2,1,0:T(8,128)}) %all-reduce.2.cloned.1.call-update) | async-done | bytes 1048592 | tf_op jit(solution)/shard_map/psum | solution.py:194
  481.4 2.3 broadcast_multiply_fusion
  (70 shorter events, 7.0 us)
Async XLA Ops:
  7.2 177.1 %copy-start = (bf16[256,256]{1,0:T(8,128)(2,1)S(1)}, bf16[256,256]{1,0:T(8,128)(2,1)}, u32[]{:S(2)}) copy-start(bf16[256,256]{1,0:T(8,128)(2,1)} %param.18) | copy-start | bytes 393220
  7.2 17.3 %copy-start.6 = (s32[512]{0:T(512)S(1)}, s32[512]{0:T(512)}, u32[]{:S(2)}) copy-start(s32[512]{0:T(512)} %param.13) | copy-start | bytes 6148
  7.2 17.3 %copy-start.5 = (s32[512,4]{0,1:T(4,128)S(1)}, s32[512,4]{0,1:T(4,128)}, u32[]{:S(2)}) copy-start(s32[512,4]{0,1:T(4,128)} %param.12) | copy-start | bytes 24580
  8.0 151.8 %collective-permute-start = (bf16[8,16,128]{2,1,0:T(8,128)(2,1)S(1)}, bf16[8,16,128]{2,1,0:T(8,128)(2,1)S(1)}, u32[]{:S(2)}, u32[]{:S(2)}) collective-permute-start(bf16[8,16,128]{2,1,0:T(8,128)(2,1)S(1)} %slice.121), channel_id=1, source_target_pairs={{0,32},{32,64},{64,96},{96,128},{128,160},{160,192},{192,224},{224... | collective-permute-start | bytes 98312 | tf_op jit(solution)/shard_map/ppermute | solution.py:13
  11.4 161.4 %all-to-all-start.2 = ((bf16[32,16,256]{2,1,0:T(8,128)(2,1)}), bf16[32,16,256]{2,1,0:T(8,128)(2,1)S(1)}, u32[]{:S(2)}, u32[]{:S(2)}) async-start(bf16[32,16,256]{2,1,0:T(8,128)(2,1)} %bitcast.20), calls=%async_computation.2 | async-start | bytes 524288 | tf_op jit(solution)/shard_map/all_to_all | solution.py:180
  24.9 13.7 %copy-start.7 = (bf16[16,129]{1,0:T(8,128)(2,1)S(1)}, bf16[16,129]{1,0:T(8,128)(2,1)}, u32[]{:S(2)}) copy-start(bf16[16,129]{1,0:T(8,128)(2,1)} %param.11) | copy-start | bytes 12388
  152.9 6.9 %copy-start.1 = (bf16[8,16,1024]{2,1,0:T(8,128)(2,1)S(1)}, bf16[8,16,1024]{2,1,0:T(8,128)(2,1)}, u32[]{:S(2)}) copy-start(bf16[8,16,1024]{2,1,0:T(8,128)(2,1)} %param.10) | copy-start | bytes 786436
  160.8 9.5 %collective-permute-start.2 = (bf16[8,16,1024]{2,1,0:T(8,128)(2,1)S(1)}, bf16[8,16,1024]{2,1,0:T(8,128)(2,1)S(1)}, u32[]{:S(2)}, u32[]{:S(2)}) collective-permute-start(bf16[8,16,1024]{2,1,0:T(8,128)(2,1)S(1)} %copy.120), channel_id=1, source_target_pairs={{1,0},{2,1},{3,2},{4,3},{5,4},{6,5},{7,6},{8,7},{9,8},{10,9},{11,1... | collective-permute-start | bytes 786440 | tf_op jit(solution)/shard_map/ppermute | solution.py:26
  163.3 8.5 %collective-permute-start.1 = (bf16[8,16,1024]{2,1,0:T(8,128)(2,1)S(1)}, bf16[8,16,1024]{2,1,0:T(8,128)(2,1)S(1)}, u32[]{:S(2)}, u32[]{:S(2)}) collective-permute-start(bf16[8,16,1024]{2,1,0:T(8,128)(2,1)S(1)} %copy.120), channel_id=1, source_target_pairs={{0,1},{1,2},{2,3},{3,4},{4,5},{5,6},{6,7},{7,8},{8,9},{9,10},{10,1... | collective-permute-start | bytes 786440 | tf_op jit(solution)/shard_map/ppermute | solution.py:24
  172.1 21.8 %copy-start.2 = (bf16[256,256]{1,0:T(8,128)(2,1)S(1)}, bf16[256,256]{1,0:T(8,128)(2,1)}, u32[]{:S(2)}) copy-start(bf16[256,256]{1,0:T(8,128)(2,1)} %param.16) | copy-start | bytes 393220
  172.1 22.1 %copy-start.3 = (bf16[256,256]{1,0:T(8,128)(2,1)S(1)}, bf16[256,256]{1,0:T(8,128)(2,1)}, u32[]{:S(2)}) copy-start(bf16[256,256]{1,0:T(8,128)(2,1)} %param.15) | copy-start | bytes 393220
  172.9 20.7 %all-to-all-start = ((bf16[32,16,256]{2,1,0:T(8,128)(2,1)}), bf16[32,16,256]{2,1,0:T(8,128)(2,1)S(1)}, u32[]{:S(2)}, u32[]{:S(2)}) async-start(bf16[32,16,256]{2,1,0:T(8,128)(2,1)} %bitcast.16), calls=%async_computation | async-start | bytes 524288 | tf_op jit(solution)/shard_map/all_to_all | solution.py:179
  184.0 297.3 %all-reduce.2.cloned.1.call-start = ((), (), s32[]{:S(2)}) async-start(), calls=%async_computation.3 | async-start | bytes 2097152 | tf_op jit(solution)/shard_map/psum | solution.py:194
  196.0 0.9 copy-start.4
Sparse Core Ops, SparseCore 0:
  206.1 275.1 all-reduce.1
where the time goes:
time: 491 us; the launch traced here: 490 us
  waiting for transfers between devices  267 us (54%)
  local copies, waits for them, and re-layouts  141 us (29%)
  starting transfers between devices  33 us (7%)
  blocking collectives  15.4 us (3%)
  between operations  14.6 us (3%)
  matrix products  10.1 us (2%)
  other arithmetic  9.12 us (2%)
    psum x1, waiting for transfers between devices, local(): summed = lax.psum(running, ('tm', 'contact'))  255 us
    gather x2, local copies, waits for them, and re-layouts, toeplitz(): picked = jnp.take(fir_taps, jnp.clip(lag_table, 0, rim_width), axis=1)  121 us
    all_to_all x1, blocking collectives, local(): lax.all_to_all(attended_groups, 'contact', split_axis=1, concat_axis=0, t...  15.4 us
    gather x2, local copies, waits for them, and re-layouts, local(): nbr_alive = jnp.take(alive_f, neighbours)  13.5 us
    all_to_all x1, starting transfers between devices, local(): lax.all_to_all(to_groups(cotangent, patch_len), 'contact', split_axis=0,...  12.9 us
    all_to_all x1, starting transfers between devices, local(): lax.all_to_all(grouped, 'contact', split_axis=0, concat_axis=1, tiled=True)  11.1 us
  transfers between devices with their start and end apart: 6, of which 4 were waited for; matrix products, arithmetic and copies ran while one was open for 30% of the time, Pallas kernels for 0%

commit v1 on v0

--- a/solution.py
+++ b/solution.py
@@ -191,7 +191,7 @@
     running, attended_groups = lax.scan(
         run_group, jnp.zeros((4, patch_len, patch_len), jnp.float32), (features, upstream)
     )
-    summed = lax.psum(running, ("tm", "contact"))
+    summed = lax.psum(lax.psum(running, "contact"), "tm")
     returned = lax.all_to_all(attended_groups, "contact", split_axis=1, concat_axis=0, tiled=True)
     attended = from_groups(returned, batch_size)
     grad_scale = (batch_size * patch_count * lax.axis_size("tm") * neighbours.shape[0]) ** (-0.5)

time: 491 us -> 713 us (1.45)
  the two profiles are of different devices: /device:TPU:24 before, /device:TPU:1 now
where the time goes in v1:
time: 713 us; the launch traced here: 712 us
  waiting for transfers between devices  483 us (68%)
  local copies, waits for them, and re-layouts  141 us (20%)
  starting transfers between devices  39 us (5%)
  blocking collectives  15.4 us (2%)
  between operations  14.6 us (2%)
  matrix products  10.1 us (1%)
  other arithmetic  9.12 us (1%)
    psum x2, waiting for transfers between devices, local(): summed = lax.psum(lax.psum(running, 'contact'), 'tm')  471 us
    gather x2, local copies, waits for them, and re-layouts, toeplitz(): picked = jnp.take(fir_taps, jnp.clip(lag_table, 0, rim_width), axis=1)  121 us
    all_to_all x1, blocking collectives, local(): lax.all_to_all(attended_groups, 'contact', split_axis=1, concat_axis=0, t...  15.4 us
  transfers between devices with their start and end apart: 7, of which 5 were waited for; matrix products, arithmetic and copies ran while one was open for 20% of the time, Pallas kernels for 0%

profile of v1, /device:TPU:1, one launch (start us, length us, event | category | flops | bytes accessed | tf_op | source)
XLA Modules:
  0.0 712.4 jit_solution(993340102872763163)
XLA Ops:
  7.2 0.8 slice.121
  8.0 12.0 %collective-permute-start = (bf16[8,16,128]{2,1,0:T(8,128)(2,1)S(1)}, bf16[8,16,128]{2,1,0:T(8,128)(2,1)S(1)}, u32[]{:S(2)}, u32[]{:S(2)}) collective-permute-start(bf16[8,16,128]{2,1,0:T(8,128)(2,1)S(1)} %slice.121), channel_id=1, source_target_pairs={{0,32},{32,64},{64,96},{96,128},{128,160},{160,192},{192,224},{224... | collective-permute-start | bytes 98312 | tf_op jit(solution)/shard_map/ppermute | solution.py:13
  20.0 1.0 fusion.132
  21.0 0.7 pad_maximum_fusion.5
  21.7 9.9 %all-to-all-start.2 = ((bf16[32,16,256]{2,1,0:T(8,128)(2,1)}), bf16[32,16,256]{2,1,0:T(8,128)(2,1)S(1)}, u32[]{:S(2)}, u32[]{:S(2)}) async-start(bf16[32,16,256]{2,1,0:T(8,128)(2,1)} %bitcast.20), calls=%async_computation.2 | async-start | bytes 524288 | tf_op jit(solution)/shard_map/all_to_all | solution.py:180
  32.2 13.2 %gather_fusion.1 = f32[2048]{0:T(1024)S(1)} fusion(f32[512]{0:T(512)S(1)} %convert_element_type.188, s32[2048]{0:T(1024)S(1)} %broadcast_clamp_fusion), kind=kCustom, calls=%fused_computation.1 | custom fusion | bytes 24576 | tf_op jit(solution)/shard_map/jit(_take)/gather | solution.py:161
  46.0 114.2 %gather_fusion = bf16[32768,16]{1,0:T(8,128)(2,1)} fusion(bf16[16,129]{0,1:T(8,128)(2,1)S(1)} %copy.116, s32[32768]{0:T(1024)S(1)} %fusion.71), kind=kCustom, calls=%fused_computation | custom fusion | bytes 2228224 | tf_op jit(solution)/shard_map/jit(_take)/gather | solution.py:45
  160.2 6.9 copy.117
  167.4 0.4 fusion.22
  168.1 1.3 collective-permute-start.2
  169.4 4.0 collective-permute-start.1
  173.6 0.8 dynamic_slice.18
  174.3 0.9 collective-permute-done.2
  175.2 1.5 collective-permute-done.1
  176.7 0.3 fusion.20
  177.1 0.7 pad_maximum_fusion.3
  177.8 11.5 %all-to-all-start = ((bf16[32,16,256]{2,1,0:T(8,128)(2,1)}), bf16[32,16,256]{2,1,0:T(8,128)(2,1)S(1)}, u32[]{:S(2)}, u32[]{:S(2)}) async-start(bf16[32,16,256]{2,1,0:T(8,128)(2,1)} %bitcast.16), calls=%async_computation | async-start | bytes 524288 | tf_op jit(solution)/shard_map/all_to_all | solution.py:179
  189.7 9.7 %all-to-all-done = bf16[32,16,256]{2,1,0:T(8,128)(2,1)S(1)} async-done(((bf16[32,16,256]{2,1,0:T(8,128)(2,1)}), bf16[32,16,256]{2,1,0:T(8,128)(2,1)S(1)}, u32[]{:S(2)}, u32[]{:S(2)}) %all-to-all-start) | async-done | bytes 262176 | tf_op jit(solution)/shard_map/all_to_all | solution.py:179
  200.3 0.4 fusion.134
  200.7 0.4 fusion.135
  201.1 0.4 fusion.136
  201.4 0.4 fusion.137
  202.2 0.5 copy-done.4
  203.8 0.3 convolution_convert_fusion.14
  204.1 0.3 convolution_convert_fusion.15
  204.9 0.3 convolution_convert_fusion.16
  205.6 0.3 convolution_convert_fusion.17
  206.1 0.4 fusion.12
  206.5 0.3 convolution_convert_fusion.18
  207.0 0.4 fusion.13
  207.4 0.3 convolution_convert_fusion.19
  207.9 0.4 fusion.14
  208.3 0.3 convolution_convert_fusion.20
  208.8 0.4 fusion.15
  209.2 0.3 convolution_convert_fusion.21
  210.0 0.3 convolution_bitcast_fusion.2
  210.2 0.3 convolution_bitcast_fusion.3
  210.5 0.3 convolution_bitcast_fusion.4
  210.8 1.0 pad_maximum_fusion
  212.1 283.4 %all-reduce.3.cloned.1.call-done = f32[4,256,256]{2,1,0:T(8,128)} async-done(((f32[4,256,256]{2,1,0:T(8,128)}), f32[4,256,256]{2,1,0:T(8,128)}) %all-reduce.3.cloned.1.call-update) | async-done | bytes 1048592 | tf_op jit(solution)/shard_map/psum | solution.py:194
  495.8 0.4 copy.146
  496.2 0.5 broadcast.198
  496.7 2.2 reduce.4
  499.0 15.4 %all_to_all.12 = bf16[32,2,2048]{2,1,0:T(2,128)(2,1)S(1)} all-to-all(bf16[32,2,2048]{2,1,0:T(2,128)(2,1)S(1)} %reshape.193), channel_id=1, replica_groups=mesh['tm'=16,'contact'=32] {'contact'}, dimensions={0} | all-to-all | bytes 524288 | tf_op jit(solution)/shard_map/all_to_all | solution.py:195
  514.4 0.3 reshape.194
  514.7 0.7 copy.142
  515.4 187.9 %all-reduce.5.cloned.1.call-done = f32[4,256,256]{2,1,0:T(8,128)} async-done(((f32[4,256,256]{2,1,0:T(8,128)}), f32[4,256,256]{2,1,0:T(8,128)}) %all-reduce.5.cloned.1.call-update) | async-done | bytes 1048592 | tf_op jit(solution)/shard_map/psum | solution.py:194
  703.3 2.3 broadcast_multiply_fusion
  (73 shorter events, 7.3 us)
Async XLA Ops:
  7.2 182.2 %copy-start = (bf16[256,256]{1,0:T(8,128)(2,1)S(1)}, bf16[256,256]{1,0:T(8,128)(2,1)}, u32[]{:S(2)}) copy-start(bf16[256,256]{1,0:T(8,128)(2,1)} %param.18) | copy-start | bytes 393220
  7.2 24.7 %copy-start.6 = (s32[512]{0:T(512)S(1)}, s32[512]{0:T(512)}, u32[]{:S(2)}) copy-start(s32[512]{0:T(512)} %param.13) | copy-start | bytes 6148
  7.2 24.7 %copy-start.5 = (s32[512,4]{0,1:T(4,128)S(1)}, s32[512,4]{0,1:T(4,128)}, u32[]{:S(2)}) copy-start(s32[512,4]{0,1:T(4,128)} %param.12) | copy-start | bytes 24580
  8.0 159.1 %collective-permute-start = (bf16[8,16,128]{2,1,0:T(8,128)(2,1)S(1)}, bf16[8,16,128]{2,1,0:T(8,128)(2,1)S(1)}, u32[]{:S(2)}, u32[]{:S(2)}) collective-permute-start(bf16[8,16,128]{2,1,0:T(8,128)(2,1)S(1)} %slice.121), channel_id=1, source_target_pairs={{0,32},{32,64},{64,96},{96,128},{128,160},{160,192},{192,224},{224... | collective-permute-start | bytes 98312 | tf_op jit(solution)/shard_map/ppermute | solution.py:13
  21.7 156.1 %all-to-all-start.2 = ((bf16[32,16,256]{2,1,0:T(8,128)(2,1)}), bf16[32,16,256]{2,1,0:T(8,128)(2,1)S(1)}, u32[]{:S(2)}, u32[]{:S(2)}) async-start(bf16[32,16,256]{2,1,0:T(8,128)(2,1)} %bitcast.20), calls=%async_computation.2 | async-start | bytes 524288 | tf_op jit(solution)/shard_map/all_to_all | solution.py:180
  32.2 13.7 %copy-start.7 = (bf16[16,129]{1,0:T(8,128)(2,1)S(1)}, bf16[16,129]{1,0:T(8,128)(2,1)}, u32[]{:S(2)}) copy-start(bf16[16,129]{1,0:T(8,128)(2,1)} %param.11) | copy-start | bytes 12388
  160.2 6.9 copy-start.1
  168.1 7.1 collective-permute-start.2
  169.4 7.3 %collective-permute-start.1 = (bf16[8,16,1024]{2,1,0:T(8,128)(2,1)S(1)}, bf16[8,16,1024]{2,1,0:T(8,128)(2,1)S(1)}, u32[]{:S(2)}, u32[]{:S(2)}) collective-permute-start(bf16[8,16,1024]{2,1,0:T(8,128)(2,1)S(1)} %copy.120), channel_id=1, source_target_pairs={{0,1},{1,2},{2,3},{3,4},{4,5},{5,6},{6,7},{7,8},{8,9},{9,10},{10,1... | collective-permute-start | bytes 786440 | tf_op jit(solution)/shard_map/ppermute | solution.py:24
  177.0 22.7 %copy-start.2 = (bf16[256,256]{1,0:T(8,128)(2,1)S(1)}, bf16[256,256]{1,0:T(8,128)(2,1)}, u32[]{:S(2)}) copy-start(bf16[256,256]{1,0:T(8,128)(2,1)} %param.16) | copy-start | bytes 393220
  177.1 23.0 %copy-start.3 = (bf16[256,256]{1,0:T(8,128)(2,1)S(1)}, bf16[256,256]{1,0:T(8,128)(2,1)}, u32[]{:S(2)}) copy-start(bf16[256,256]{1,0:T(8,128)(2,1)} %param.15) | copy-start | bytes 393220
  177.8 21.6 %all-to-all-start = ((bf16[32,16,256]{2,1,0:T(8,128)(2,1)}), bf16[32,16,256]{2,1,0:T(8,128)(2,1)S(1)}, u32[]{:S(2)}, u32[]{:S(2)}) async-start(bf16[32,16,256]{2,1,0:T(8,128)(2,1)} %bitcast.16), calls=%async_computation | async-start | bytes 524288 | tf_op jit(solution)/shard_map/all_to_all | solution.py:179
  189.3 306.2 %all-reduce.3.cloned.1.call-start = ((), (), s32[]{:S(2)}) async-start(), calls=%async_computation.3 | async-start | bytes 2097152 | tf_op jit(solution)/shard_map/psum | solution.py:194
  201.8 0.9 copy-start.4
  211.9 491.5 %all-reduce.5.cloned.1.call-start = ((), (), s32[]{:S(2)}) async-start(), calls=%async_computation.4 | async-start | bytes 2097152 | tf_op jit(solution)/shard_map/psum | solution.py:194
Sparse Core Ops, SparseCore 0:
  212.0 283.4 all-reduce.2
  498.7 204.6 all-reduce.4
